TPU v7x, 512 devices: a whole 4x4x16 slice. The times are simulated.
512 devices in a mesh: pair: 64 (over x, y, z_hi), sector: 8 (over z_lo, core).
Axes of the slice: x: 4, y: 4, z: 16 (z_hi: 4, z_lo: 4; z = z_hi * 4 + z_lo), core: 2. Of those that a mesh axis runs over, the one named last changes fastest.
Arguments:
- site_tensor: bfloat16 [4, 16, 128, 128], P(None, 'sector', 'pair'), may hold values from -0.5 to 0.5
- operators: bfloat16 [1536, 16, 128, 128], P('pair', 'sector'), may hold values from -6 to 6
- one_index: bfloat16 [128, 16, 128, 128], P('pair', 'sector'), may hold values from -6 to 6
- weights: bfloat16 [1536, 128], P('pair'), may hold values from -1 to 1
- comp_charge: int32 [1536], P('pair'), may hold values from 0 to 2
- one_charge: int32 [128], replicated, may hold values from 0 to 2
- sector_size: int32 [16], replicated, may hold values from 1 to 128, 1280 in all
- coupling: int32 [16, 4], replicated, may hold values from 0 to 16, as said below
Outputs:
- renormalized: bfloat16 [1536, 16, 128, 128], P('pair', 'sector')
Inputs may be any that keep to these rules, and one draw needn't show every extreme that they name: coupling[s, t] = min(s + c[t], 16) where c is an arrangement of the charges 0, 1, 1, 2 over the 4 orbital states; the value 16 marks a dropped combination.
All inputs are finite; a program needn't handle non-finite values.
Results may differ from a plain program's by a relative error of at most 0.007.
Values may be sent and summed in bfloat16 or wider, within the bound.
No kernel may reach another device: no remote copies, remote signals or barrier semaphores. Data moves between devices by JAX's collectives and lax.ppermute only.
A program may use at most 64 MiB of HBM per device.

v0:
```python
import jax
import jax.numpy as jnp
from jax import lax
from jax.sharding import PartitionSpec as P


def from_behind(value, axis, steps):
    count = lax.axis_size(axis)
    initial, last = (max(0, -steps), min(count, count - steps))
    return lax.ppermute(value, axis, [(source, source + steps) for source in range(initial, last)])


def body(
    site_tensor, operators, one_index, weights, comp_charge, one_charge, sector_size, coupling
):
    sec_local = operators.shape[1]
    block_size = operators.shape[2]
    ops_local = operators.shape[0]
    states = site_tensor.shape[0]
    total_sectors = sec_local * lax.axis_size("sector")
    first_sector = lax.axis_index("sector") * sec_local
    full_site = lax.all_gather(site_tensor, "pair", axis=2, tiled=True)
    positions = jnp.arange(block_size, dtype=jnp.int32)
    own_sizes = lax.dynamic_slice_in_dim(sector_size, first_sector, sec_local)
    live_rows = positions[None, :] < own_sizes[:, None]
    own_site = jnp.where(live_rows[None, :, :, None], full_site, jnp.zeros((), jnp.bfloat16))
    upper_blocks = from_behind(own_site, "sector", -1)
    right_pool = jnp.concatenate([own_site, upper_blocks], axis=1)
    matching = comp_charge[:, None] == one_charge[None, :]
    coef = jnp.where(matching, weights, jnp.zeros((), jnp.bfloat16))
    shard_piece = lax.all_gather(one_index, "pair", axis=0, tiled=True)
    piece_rows = shard_piece.shape[0]
    flattened = shard_piece.reshape(piece_rows, -1)
    summed = jnp.dot(coef, flattened, preferred_element_type=jnp.float32)
    combined = (operators.astype(jnp.float32) + summed.reshape(operators.shape)).astype(
        jnp.bfloat16
    )
    state_charge = coupling[0]
    pool_count = right_pool.shape[1]
    global_right = (
        first_sector + jnp.arange(sec_local, dtype=jnp.int32)[None, :] + comp_charge[:, None]
    )
    in_range = global_right < total_sectors
    pool_index = jnp.clip(global_right - first_sector, 0, pool_count - 1)
    gathered_out = jnp.zeros((ops_local, sec_local + 2, block_size, block_size), jnp.float32)
    for local_state in range(states):
        right_blocks = right_pool[local_state][pool_index]
        right_blocks = jnp.where(
            in_range[:, :, None, None], right_blocks, jnp.zeros((), jnp.bfloat16)
        )
        partial_value = jnp.einsum(
            "ksij,ksjc->ksic", combined, right_blocks, preferred_element_type=jnp.float32
        ).astype(jnp.bfloat16)
        contrib = jnp.einsum(
            "sia,ksic->ksac",
            own_site[local_state],
            partial_value,
            preferred_element_type=jnp.float32,
        )
        offset = state_charge[local_state]
        current = lax.dynamic_slice_in_dim(gathered_out, offset, sec_local, 1)
        gathered_out = lax.dynamic_update_slice_in_dim(gathered_out, current + contrib, offset, 1)
    carried = from_behind(gathered_out[:, sec_local:].astype(jnp.bfloat16), "sector", 1).astype(
        jnp.float32
    )
    landed = gathered_out[:, :sec_local].at[:, :2].add(carried)
    return landed.astype(jnp.bfloat16)


def solution(mesh):
    return jax.shard_map(
        body,
        mesh=mesh,
        in_specs=(
            P(None, "sector", "pair", None),
            P("pair", "sector", None, None),
            P("pair", "sector", None, None),
            P("pair", None),
            P("pair"),
            P(),
            P(),
            P(),
        ),
        out_specs=P("pair", "sector", None, None),
        check_vma=False,
    )
```

profile of v0, /device:TPU:38, one launch (start us, length us, event | category | flops | bytes accessed | tf_op | source)
XLA Modules:
  0.0 383.1 jit_solution(11426421221952369991)
XLA Ops:
  6.5 0.0 all-gather.2.cloned.1.call-start
  6.5 0.7 all-gather.2.cloned.1.call-update
  7.3 0.7 copy.17
  8.0 0.7 dynamic_slice.12
  8.7 249.5 %all_gather.7 = bf16[4,2,128,128]{3,0,1,2:T(4,128)(2,1)S(1)} all-gather(bf16[4,2,2,128]{3,0,1,2:T(4,128)(2,1)S(1)} %copy.17), channel_id=1, replica_groups=mesh['pair'=64,'sector'=8] {'pair'}, dimensions={2}, use_global_device_ids=true | all-gather | bytes 266240 | tf_op jit(solution)/shard_map/all_gather | solution.py:22
  258.2 0.1 iota_compare_fusion
  258.3 0.1 copy_select_fusion.16
  258.4 1.9 collective-permute-start
  260.3 0.7 compare_select_fusion
  261.1 0.1 reshape.165
  261.2 1.4 fusion.49
  270.1 0.7 add_compare_fusion
  270.9 0.0 collective-permute-done
  270.9 1.9 gather_fusion
  272.9 1.9 gather_fusion.1
  274.8 2.0 gather_fusion.2
  276.8 0.8 gather_fusion.3
  277.6 0.0 copy-start
  277.6 0.0 copy-start.1
  277.6 0.0 copy-start.2
  277.7 0.0 all-gather.2.cloned.1.call-done
  277.7 12.7 %copy.41 = bf16[128,2,128,128]{0,3,2,1:T(8,128)(2,1)} copy(bf16[128,2,128,128]{3,2,1,0:T(8,128)(2,1)} %all-gather.2.cloned.1.call-done) | data formatting | bytes 16777216 | tf_op jit(solution)/shard_map/reshape | solution.py:33
  290.4 0.0 copy-done
  290.4 0.0 copy-done.1
  290.4 0.0 copy-done.2
  290.4 8.3 %add_convert_fusion = bf16[24,2,128,128]{3,0,2,1:T(8,128)(2,1)S(1)} fusion(bf16[128,2,128,128]{0,3,2,1:T(8,128)(2,1)} %copy.41, bf16[24,2,128,128]{3,2,1,0:T(8,128)(2,1)} %param.13, bf16[24,128]{1,0:T(8,128)(2,1)S(1)} %copy-done, s32[128]{0:T(128)S(1)} %copy-done.2, s32[24]{0:T(128)S(1)} %copy-done.1), kind=kOutput, calls=%fused_computation.16 | convolution fusion | flops 203692032 | bytes 11541088 | tf_op jit(solution)/shard_map/dot_general | solution.py:34
  298.7 3.5 broadcast_in_dim.58
  302.1 4.1 %bitcast_dynamic-update-slice_fusion = f32[24,4,128,128]{2,3,0,1:T(8,128)} fusion(f32[24,4,128,128]{2,3,0,1:T(8,128)} %broadcast_in_dim.58, s32[]{:T(128)S(6)} %select_n.57, bf16[24,2,128,128]{3,2,1,0:T(8,128)(2,1)} %bitcast.73, pred[24,2]{0,1:T(4,128)(4,1)S(1)} %add_compare_fusion, bf16[24,2,128,128]{3,0,2,1:T(8,128)(2,1)S(1)} %add_convert_fusion, ...), kind=kOutput, calls=%fused_computation.15 | convolution fusion | flops 404226048 | bytes 6357508 | tf_op jit(solution)/shard_map/sia,ksic->ksac/dot_general | solution.py:54
  306.2 5.1 %fusion.5 = f32[24,4,128,128]{2,3,0,1:T(8,128)} fusion(f32[24,4,128,128]{2,3,0,1:T(8,128)} %bitcast_dynamic-update-slice_fusion, s32[]{:T(128)S(6)} %select_n.58, bf16[24,2,128,128]{3,2,1,0:T(8,128)(2,1)} %bitcast.72, pred[24,2]{0,1:T(4,128)(4,1)S(1)} %add_compare_fusion, bf16[24,2,128,128]{3,0,2,1:T(8,128)(2,1)S(1)} %add_convert_fusion, ...), kind=kOutput, calls=%fused_computation.14 | convolution fusion | flops 405012480 | bytes 9503236 | tf_op jit(solution)/shard_map/sia,ksic->ksac/dot_general | solution.py:54
  311.3 5.1 %fusion.4 = f32[24,4,128,128]{2,3,0,1:T(8,128)} fusion(f32[24,4,128,128]{2,3,0,1:T(8,128)} %fusion.5, s32[]{:T(128)S(6)} %select_n.60, bf16[24,2,128,128]{3,2,1,0:T(8,128)(2,1)} %bitcast.71, pred[24,2]{0,1:T(4,128)(4,1)S(1)} %add_compare_fusion, bf16[24,2,128,128]{3,0,2,1:T(8,128)(2,1)S(1)} %add_convert_fusion, ...), kind=kOutput, calls=%fused_computation.12 | convolution fusion | flops 405012480 | bytes 9503236 | tf_op jit(solution)/shard_map/sia,ksic->ksac/dot_general | solution.py:54
  316.3 4.6 %fusion.3 = f32[24,4,128,128]{2,3,0,1:T(8,128)} fusion(f32[24,4,128,128]{2,3,0,1:T(8,128)} %fusion.4, s32[]{:T(128)S(6)} %select_n.62, bf16[24,2,128,128]{3,2,1,0:T(8,128)(2,1)S(1)} %bitcast.70, pred[24,2]{0,1:T(4,128)(4,1)S(1)} %add_compare_fusion, bf16[24,2,128,128]{3,0,2,1:T(8,128)(2,1)S(1)} %add_convert_fusion, ...), kind=kOutput, calls=%fused_computation.10 | convolution fusion | flops 405012480 | bytes 9503236 | tf_op jit(solution)/shard_map/sia,ksic->ksac/dot_general | solution.py:54
  321.0 2.1 slice.146
  323.1 2.4 collective-permute-start.1
  325.5 46.7 %collective-permute-done.1 = bf16[24,2,128,128]{2,3,0,1:T(8,128)(2,1)S(1)} collective-permute-done((bf16[24,2,128,128]{2,3,0,1:T(8,128)(2,1)S(1)}, bf16[24,2,128,128]{2,3,0,1:T(8,128)(2,1)S(1)}, u32[]{:S(2)}, u32[]{:S(2)}) %collective-permute-start.1) | collective-permute-done | bytes 1572896 | tf_op jit(solution)/shard_map/ppermute | solution.py:10
  372.3 2.4 fusion.2
  374.7 1.6 copy.31
  (3 shorter events, 0.1 us)
Async XLA Ops:
  6.5 271.1 %all-gather.2.cloned.1.call-start = ((), (), s32[]{:S(2)}) async-start(), calls=%async_computation | async-start | bytes 8519680 | tf_op jit(solution)/shard_map/all_gather | solution.py:31
  258.4 12.5 %collective-permute-start = (bf16[4,2,128,128]{3,2,1,0:T(8,128)(2,1)S(1)}, bf16[4,2,128,128]{3,2,1,0:T(8,128)(2,1)S(1)}, u32[]{:S(2)}, u32[]{:S(2)}) collective-permute-start(bf16[4,2,128,128]{3,2,1,0:T(8,128)(2,1)S(1)} %copy_select_fusion.16), channel_id=1, source_target_pairs={{1,0},{2,1},{3,2},{4,3},{5,4},{6,5},{7,6},{9,8},{10,9},{11,10},{12... | collective-permute-start | bytes 786440 | tf_op jit(solution)/shard_map/ppermute | solution.py:10
  277.6 12.8 %copy-start = (bf16[24,128]{1,0:T(8,128)(2,1)S(1)}, bf16[24,128]{1,0:T(8,128)(2,1)}, u32[]{:S(2)}) copy-start(bf16[24,128]{1,0:T(8,128)(2,1)} %param.15) | copy-start | bytes 18436
  277.6 12.7 %copy-start.1 = (s32[24]{0:T(128)S(1)}, s32[24]{0:T(128)}, u32[]{:S(2)}) copy-start(s32[24]{0:T(128)} %param.16) | copy-start | bytes 292
  277.6 12.7 %copy-start.2 = (s32[128]{0:T(128)S(1)}, s32[128]{0:T(128)}, u32[]{:S(2)}) copy-start(s32[128]{0:T(128)} %param.17) | copy-start | bytes 1540
  323.1 49.1 %collective-permute-start.1 = (bf16[24,2,128,128]{2,3,0,1:T(8,128)(2,1)S(1)}, bf16[24,2,128,128]{2,3,0,1:T(8,128)(2,1)S(1)}, u32[]{:S(2)}, u32[]{:S(2)}) collective-permute-start(bf16[24,2,128,128]{2,3,0,1:T(8,128)(2,1)S(1)} %slice.146), channel_id=1, source_target_pairs={{0,1},{1,2},{2,3},{3,4},{4,5},{5,6},{6,7},{8,9},{9,10},{10,11},{11... | collective-permute-start | bytes 4718600 | tf_op jit(solution)/shard_map/ppermute | solution.py:10
Sparse Core Ops, SparseCore 0:
  11.5 168.6 all-gather.1
where the time goes:
time: 384 us; the launch traced here: 383 us
  blocking collectives  250 us (65%)
  waiting for transfers between devices  47.5 us (12%)
  local copies, waits for them, and re-layouts  29.5 us (8%)
  matrix products  27.1 us (7%)
  between operations  21.1 us (5%)
  starting transfers between devices  4.33 us (1%)
  other arithmetic  4.1 us (1%)
    all_gather x1, blocking collectives, body(): full_site = lax.all_gather(site_tensor, 'pair', axis=2, tiled=True)  250 us
    ppermute x2, waiting for transfers between devices, from_behind(): lax.ppermute(value, axis, [(source, source + steps) for source in range(i...  46.7 us
    dot_general x4, matrix products, body(): jnp.einsum('sia,ksic->ksac', own_site[local_state], partial_value, prefer...  18.9 us
    reshape x1, local copies, waits for them, and re-layouts, body(): flattened = shard_piece.reshape(piece_rows, -1)  12.7 us
    dot_general x1, matrix products, body(): summed = jnp.dot(coef, flattened, preferred_element_type=jnp.float32)  8.28 us
  transfers between devices with their start and end apart: 3, of which 1 were waited for; matrix products, arithmetic and copies ran while one was open for 3% of the time, Pallas kernels for 0%

commit v1 on v0

--- a/solution.py
+++ b/solution.py
@@ -19,7 +19,9 @@
     states = site_tensor.shape[0]
     total_sectors = sec_local * lax.axis_size("sector")
     first_sector = lax.axis_index("sector") * sec_local
-    full_site = lax.all_gather(site_tensor, "pair", axis=2, tiled=True)
+    full_site = jnp.concatenate(
+        lax.all_to_all(jnp.stack([site_tensor] * lax.axis_size("pair")), "pair", 0, 0), axis=2
+    )
     positions = jnp.arange(block_size, dtype=jnp.int32)
     own_sizes = lax.dynamic_slice_in_dim(sector_size, first_sector, sec_local)
     live_rows = positions[None, :] < own_sizes[:, None]

time: 384 us -> 291 us (0.76)
  the two profiles are of different devices: /device:TPU:38 before, /device:TPU:1 now
where the time goes in v1:
time: 291 us; the launch traced here: 290 us
  waiting for transfers between devices  177 us (61%)
  starting transfers between devices  31.1 us (11%)
  local copies, waits for them, and re-layouts  30.5 us (10%)
  matrix products  27.1 us (9%)
  between operations  20.8 us (7%)
  other arithmetic  3.44 us (1%)
    all_gather x1, waiting for transfers between devices, body(): shard_piece = lax.all_gather(one_index, 'pair', axis=0, tiled=True)  140 us
    all_to_all x1, starting transfers between devices, body(): lax.all_to_all(jnp.stack([site_tensor] * lax.axis_size('pair')), 'pair',...  21.7 us
    ppermute x2, waiting for transfers between devices, from_behind(): lax.ppermute(value, axis, [(source, source + steps) for source in range(i...  21 us
    dot_general x4, matrix products, body(): jnp.einsum('sia,ksic->ksac', own_site[local_state], partial_value, prefer...  18.8 us
    all_to_all x1, waiting for transfers between devices, body(): lax.all_to_all(jnp.stack([site_tensor] * lax.axis_size('pair')), 'pair',...  15.1 us
    reshape x1, local copies, waits for them, and re-layouts, body(): flattened = shard_piece.reshape(piece_rows, -1)  12.6 us
    ppermute x2, starting transfers between devices, from_behind(): lax.ppermute(value, axis, [(source, source + steps) for source in range(i...  9.41 us
    dot_general x1, matrix products, body(): summed = jnp.dot(coef, flattened, preferred_element_type=jnp.float32)  8.28 us
  transfers between devices with their start and end apart: 4, of which 4 were waited for; matrix products, arithmetic and copies ran while one was open for 4% of the time, Pallas kernels for 0%

profile of v1, /device:TPU:1, one launch (start us, length us, event | category | flops | bytes accessed | tf_op | source)
XLA Modules:
  0.0 289.9 jit_solution(11286528494248785750)
XLA Ops:
  6.5 0.0 copy-start.1
  6.5 0.0 all-gather.2.cloned.1.call-start
  6.5 0.7 all-gather.2.cloned.1.call-update
  7.3 1.5 stack.2
  8.8 21.7 %all-to-all-start = ((bf16[64,4,2,2,128]{4,3,2,1,0:T(2,128)(2,1)}), bf16[64,4,2,2,128]{4,3,2,1,0:T(2,128)(2,1)S(1)}, u32[]{:S(2)}, u32[]{:S(2)}) async-start(bf16[64,4,2,2,128]{4,3,2,1,0:T(2,128)(2,1)} %stack.2), calls=%async_computation | async-start | bytes 524288 | tf_op jit(solution)/shard_map/all_to_all | solution.py:23
  30.5 0.7 compare_select_fusion
  31.3 0.1 reshape.175
  31.4 0.7 dynamic_slice.12
  32.1 1.4 fusion.49
  33.5 0.1 iota_compare_fusion
  33.6 15.1 %all-to-all-done = bf16[64,4,2,2,128]{4,3,2,1,0:T(2,128)(2,1)S(1)} async-done(((bf16[64,4,2,2,128]{4,3,2,1,0:T(2,128)(2,1)}), bf16[64,4,2,2,128]{4,3,2,1,0:T(2,128)(2,1)S(1)}, u32[]{:S(2)}, u32[]{:S(2)}) %all-to-all-start) | async-done | bytes 262176 | tf_op jit(solution)/shard_map/all_to_all | solution.py:23
  48.7 0.2 copy.17
  48.9 0.1 broadcast_select_fusion
  49.0 7.5 %collective-permute-start = (bf16[4,2,128,128]{3,2,1,0:T(8,128)(2,1)S(1)}, bf16[4,2,128,128]{3,2,1,0:T(8,128)(2,1)S(1)}, u32[]{:S(2)}, u32[]{:S(2)}) collective-permute-start(bf16[4,2,128,128]{3,2,1,0:T(8,128)(2,1)S(1)} %broadcast_select_fusion), channel_id=1, source_target_pairs={{1,0},{2,1},{3,2},{4,3},{5,4},{6,5},{7,6},{9,8},{10,9},{11,10},{12... | collective-permute-start | bytes 786440 | tf_op jit(solution)/shard_map/ppermute | solution.py:10
  63.8 0.0 copy-done.1
  63.8 0.1 add_compare_fusion
  63.9 3.7 %collective-permute-done = bf16[4,2,128,128]{3,2,1,0:T(8,128)(2,1)S(1)} collective-permute-done((bf16[4,2,128,128]{3,2,1,0:T(8,128)(2,1)S(1)}, bf16[4,2,128,128]{3,2,1,0:T(8,128)(2,1)S(1)}, u32[]{:S(2)}, u32[]{:S(2)}) %collective-permute-start) | collective-permute-done | bytes 262176 | tf_op jit(solution)/shard_map/ppermute | solution.py:10
  67.6 1.9 gather_fusion
  69.5 2.0 gather_fusion.1
  71.5 2.0 gather_fusion.2
  73.5 0.8 gather_fusion.3
  74.3 0.0 copy-start
  74.3 0.0 copy-start.2
  74.3 140.2 %all-gather.2.cloned.1.call-done = bf16[128,2,128,128]{3,2,1,0:T(8,128)(2,1)} async-done(((bf16[2,2,128,128]{3,2,1,0:T(8,128)(2,1)}), bf16[128,2,128,128]{3,2,1,0:T(8,128)(2,1)}) %all-gather.2.cloned.1.call-update) | async-done | bytes 8388624 | tf_op jit(solution)/shard_map/all_gather | solution.py:33
  214.5 12.6 %copy.40 = bf16[128,2,128,128]{0,3,2,1:T(8,128)(2,1)} copy(bf16[128,2,128,128]{3,2,1,0:T(8,128)(2,1)} %all-gather.2.cloned.1.call-done) | data formatting | bytes 16777216 | tf_op jit(solution)/shard_map/reshape | solution.py:35
  227.1 0.0 copy-done
  227.1 0.0 copy-done.2
  227.1 8.3 %add_convert_fusion = bf16[24,2,128,128]{3,0,2,1:T(8,128)(2,1)S(1)} fusion(bf16[128,2,128,128]{0,3,2,1:T(8,128)(2,1)} %copy.40, bf16[24,2,128,128]{3,2,1,0:T(8,128)(2,1)} %param.13, bf16[24,128]{1,0:T(8,128)(2,1)S(1)} %copy-done, s32[128]{0:T(128)S(1)} %copy-done.2, s32[24]{0:T(128)S(1)} %copy-done.1), kind=kOutput, calls=%fused_computation.16 | convolution fusion | flops 203692032 | bytes 11541088 | tf_op jit(solution)/shard_map/dot_general | solution.py:36
  235.4 3.4 %broadcast_in_dim.58 = f32[24,4,128,128]{2,3,0,1:T(8,128)} broadcast(f32[]{:T(128)} %constant.48.clone.1), dimensions={} | broadcast | bytes 6291460 | tf_op jit(solution)/shard_map/broadcast_in_dim | solution.py:47
  238.9 4.1 %bitcast_dynamic-update-slice_fusion = f32[24,4,128,128]{2,3,0,1:T(8,128)} fusion(f32[24,4,128,128]{2,3,0,1:T(8,128)} %broadcast_in_dim.58, s32[]{:T(128)S(6)} %select_n.57, bf16[24,2,128,128]{3,2,1,0:T(8,128)(2,1)} %bitcast.75, pred[24,2]{0,1:T(4,128)(4,1)S(1)} %add_compare_fusion, bf16[24,2,128,128]{3,0,2,1:T(8,128)(2,1)S(1)} %add_convert_fusion, ...), kind=kOutput, calls=%fused_computation.15 | convolution fusion | flops 404226048 | bytes 6357508 | tf_op jit(solution)/shard_map/sia,ksic->ksac/dot_general | solution.py:56
  242.9 5.1 %fusion.5 = f32[24,4,128,128]{2,3,0,1:T(8,128)} fusion(f32[24,4,128,128]{2,3,0,1:T(8,128)} %bitcast_dynamic-update-slice_fusion, s32[]{:T(128)S(6)} %select_n.58, bf16[24,2,128,128]{3,2,1,0:T(8,128)(2,1)} %bitcast.74, pred[24,2]{0,1:T(4,128)(4,1)S(1)} %add_compare_fusion, bf16[24,2,128,128]{3,0,2,1:T(8,128)(2,1)S(1)} %add_convert_fusion, ...), kind=kOutput, calls=%fused_computation.14 | convolution fusion | flops 405012480 | bytes 9503236 | tf_op jit(solution)/shard_map/sia,ksic->ksac/dot_general | solution.py:56
  248.0 5.0 %fusion.4 = f32[24,4,128,128]{2,3,0,1:T(8,128)} fusion(f32[24,4,128,128]{2,3,0,1:T(8,128)} %fusion.5, s32[]{:T(128)S(6)} %select_n.60, bf16[24,2,128,128]{3,2,1,0:T(8,128)(2,1)} %bitcast.73, pred[24,2]{0,1:T(4,128)(4,1)S(1)} %add_compare_fusion, bf16[24,2,128,128]{3,0,2,1:T(8,128)(2,1)S(1)} %add_convert_fusion, ...), kind=kOutput, calls=%fused_computation.12 | convolution fusion | flops 405012480 | bytes 9503236 | tf_op jit(solution)/shard_map/sia,ksic->ksac/dot_general | solution.py:56
  253.1 4.6 %fusion.3 = f32[24,4,128,128]{2,3,0,1:T(8,128)} fusion(f32[24,4,128,128]{2,3,0,1:T(8,128)} %fusion.4, s32[]{:T(128)S(6)} %select_n.62, bf16[24,2,128,128]{3,2,1,0:T(8,128)(2,1)S(1)} %bitcast.72, pred[24,2]{0,1:T(4,128)(4,1)S(1)} %add_compare_fusion, bf16[24,2,128,128]{3,0,2,1:T(8,128)(2,1)S(1)} %add_convert_fusion, ...), kind=kOutput, calls=%fused_computation.10 | convolution fusion | flops 405012480 | bytes 9503236 | tf_op jit(solution)/shard_map/sia,ksic->ksac/dot_general | solution.py:56
  257.7 2.1 slice.146
  259.8 1.9 collective-permute-start.1
  261.8 17.3 %collective-permute-done.1 = bf16[24,2,128,128]{2,3,0,1:T(8,128)(2,1)S(1)} collective-permute-done((bf16[24,2,128,128]{2,3,0,1:T(8,128)(2,1)S(1)}, bf16[24,2,128,128]{2,3,0,1:T(8,128)(2,1)S(1)}, u32[]{:S(2)}, u32[]{:S(2)}) %collective-permute-start.1) | collective-permute-done | bytes 1572896 | tf_op jit(solution)/shard_map/ppermute | solution.py:10
  279.1 2.4 fusion.2
  281.5 1.6 copy.30
  (3 shorter events, 0.1 us)
Async XLA Ops:
  6.5 57.2 %copy-start.1 = (s32[24]{0:T(128)S(1)}, s32[24]{0:T(128)}, u32[]{:S(2)}) copy-start(s32[24]{0:T(128)} %param.16) | copy-start | bytes 292
  6.5 207.9 %all-gather.2.cloned.1.call-start = ((), (), s32[]{:S(2)}) async-start(), calls=%async_computation.1 | async-start | bytes 8519680 | tf_op jit(solution)/shard_map/all_gather | solution.py:33
  8.8 39.9 %all-to-all-start = ((bf16[64,4,2,2,128]{4,3,2,1,0:T(2,128)(2,1)}), bf16[64,4,2,2,128]{4,3,2,1,0:T(2,128)(2,1)S(1)}, u32[]{:S(2)}, u32[]{:S(2)}) async-start(bf16[64,4,2,2,128]{4,3,2,1,0:T(2,128)(2,1)} %stack.2), calls=%async_computation | async-start | bytes 524288 | tf_op jit(solution)/shard_map/all_to_all | solution.py:23
  49.0 18.6 %collective-permute-start = (bf16[4,2,128,128]{3,2,1,0:T(8,128)(2,1)S(1)}, bf16[4,2,128,128]{3,2,1,0:T(8,128)(2,1)S(1)}, u32[]{:S(2)}, u32[]{:S(2)}) collective-permute-start(bf16[4,2,128,128]{3,2,1,0:T(8,128)(2,1)S(1)} %broadcast_select_fusion), channel_id=1, source_target_pairs={{1,0},{2,1},{3,2},{4,3},{5,4},{6,5},{7,6},{9,8},{10,9},{11,10},{12... | collective-permute-start | bytes 786440 | tf_op jit(solution)/shard_map/ppermute | solution.py:10
  74.3 152.8 %copy-start = (bf16[24,128]{1,0:T(8,128)(2,1)S(1)}, bf16[24,128]{1,0:T(8,128)(2,1)}, u32[]{:S(2)}) copy-start(bf16[24,128]{1,0:T(8,128)(2,1)} %param.15) | copy-start | bytes 18436
  74.3 152.8 %copy-start.2 = (s32[128]{0:T(128)S(1)}, s32[128]{0:T(128)}, u32[]{:S(2)}) copy-start(s32[128]{0:T(128)} %param.17) | copy-start | bytes 1540
  259.8 19.3 %collective-permute-start.1 = (bf16[24,2,128,128]{2,3,0,1:T(8,128)(2,1)S(1)}, bf16[24,2,128,128]{2,3,0,1:T(8,128)(2,1)S(1)}, u32[]{:S(2)}, u32[]{:S(2)}) collective-permute-start(bf16[24,2,128,128]{2,3,0,1:T(8,128)(2,1)S(1)} %slice.146), channel_id=1, source_target_pairs={{0,1},{1,2},{2,3},{3,4},{4,5},{5,6},{6,7},{8,9},{9,10},{10,11},{11... | collective-permute-start | bytes 4718600 | tf_op jit(solution)/shard_map/ppermute | solution.py:10
Sparse Core Ops, SparseCore 0:
  11.5 202.9 all-gather.1
